TPU v7x, 32 devices: a whole 2x2x4 slice. The times are simulated.
32 devices in a mesh: narrow: 2 (over y), wide: 16 (over z, x, core).
Axes of the slice: x: 2, y: 2, z: 4, core: 2. Of those that a mesh axis runs over, the one named last changes fastest.
Arguments:
- tokens: bfloat16 [2, 16384, 768], P(None, ('narrow', 'wide')), may hold values from -6 to 6
- image_ids: int32 [2, 16384], P(None, ('narrow', 'wide')), may hold values from -1 to 1, as said below
- cotangent: bfloat16 [2, 16384, 768], P(None, ('narrow', 'wide')), may hold values from -6 to 6
- w_joined: bfloat16 [768, 5376], P('wide'), may hold values from -0.21875 to 0.21875
- w_out: bfloat16 [768, 768], P('wide'), may hold values from -1 to 1
- w_mlp: bfloat16 [3072, 768], P('wide'), may hold values from -0.109375 to 0.109375
- norm_gain: bfloat16 [768], P('wide'), may hold values from 0.5 to 1.5
- bias_attn: bfloat16 [1536], P('wide'), may hold values from -1.1953125 to 1.1953125
- bias_mlp: bfloat16 [3072], P('wide'), may hold values from -1.1953125 to 1.1953125
- bias_out: bfloat16 [768], P('wide'), may hold values from -1.1953125 to 1.1953125
Outputs:
- block_out: bfloat16 [2, 16384, 768], P(None, ('narrow', 'wide'))
- d_tokens: bfloat16 [2, 16384, 768], P(None, ('narrow', 'wide'))
- grad_joined: float32 [768, 5376], P('wide')
- grad_out: float32 [768, 768], P('wide')
- grad_mlp: float32 [3072, 768], P('wide')
- grad_gain: float32 [768], P('wide')
- grad_bias_attn: float32 [1536], P('wide')
- grad_bias_mlp: float32 [3072], P('wide')
- grad_bias_out: float32 [768], P('wide')
Inputs may be any that keep to these rules, and one draw needn't show every extreme that they name: `image_ids`: each block of 512 consecutive tokens (one device's share of a micro-batch) holds either one image of 512 tokens, all with id 0, or 2 images of 196 tokens in order with ids 0, 1, ..., followed by padding tokens with id -1. Every micro-batch has blocks of both kinds.
All inputs are finite; a program needn't handle non-finite values.
Results may differ from a plain program's by a relative error of at most 0.0083.
Values may be sent and summed in bfloat16 or wider, within the bound.
No kernel may reach another device: no remote copies, remote signals or barrier semaphores. Data moves between devices by JAX's collectives and lax.ppermute only.
A program may use at most 192 MiB of HBM per device.

v0:
```python
import jax
import jax.numpy as jnp
from jax import lax
from jax.sharding import PartitionSpec as P

HEADS = 12
norm_eps = 1e-06
masked_score = -1e30


def gelu_tanh(inputs):
    inner = 0.7978845608028654 * (inputs + 0.044715 * inputs * inputs * inputs)
    return 0.5 * inputs * (1.0 + jnp.tanh(inner))


def masked_scores(query_rows, key_rows, same_image, score_scale):
    raw_scores = (
        jnp.einsum("qhe,khe->hqk", query_rows, key_rows, preferred_element_type=jnp.float32)
        * score_scale
    )
    return jnp.where(same_image[None], raw_scores, masked_score)


def forward_block(block_rows, block_ids, gathered):
    w_joined, w_out, w_mlp, norm_gain, bias_attn, bias_mlp, bias_out = gathered
    block_len, model_width = block_rows.shape
    head_count = HEADS
    head_size = model_width // head_count
    score_scale = head_size ** (-0.5)
    inputs = block_rows.astype(jnp.float32)
    row_mean = jnp.mean(inputs, axis=1, keepdims=True)
    centered = inputs - row_mean
    inverse_std = lax.rsqrt(jnp.mean(centered * centered, axis=1, keepdims=True) + norm_eps)
    standard = centered * inverse_std
    normed = (standard * norm_gain.astype(jnp.float32)).astype(jnp.bfloat16)
    bias_full = jnp.concatenate(
        [
            bias_attn[:model_width],
            jnp.zeros((model_width,), jnp.bfloat16),
            bias_attn[model_width:],
            bias_mlp,
        ]
    ).astype(jnp.float32)
    joined = jnp.dot(normed, w_joined, preferred_element_type=jnp.float32) + bias_full
    attn_part = joined[:, : 3 * model_width].astype(jnp.bfloat16)
    pre_act = joined[:, 3 * model_width :]
    query_rows = attn_part[:, :model_width].reshape(block_len, head_count, head_size)
    key_rows = attn_part[:, model_width : 2 * model_width].reshape(block_len, head_count, head_size)
    value_rows = attn_part[:, 2 * model_width :].reshape(block_len, head_count, head_size)
    same_image = block_ids[:, None] == block_ids[None, :]
    scores = masked_scores(query_rows, key_rows, same_image, score_scale)
    row_max = jnp.max(scores, axis=2, keepdims=True)
    exponents = jnp.exp(scores - row_max)
    row_total = jnp.sum(exponents, axis=2, keepdims=True)
    probs_low = (exponents / row_total).astype(jnp.bfloat16)
    log_total = row_max + jnp.log(row_total)
    attended = jnp.einsum("hqk,khe->qhe", probs_low, value_rows, preferred_element_type=jnp.float32)
    attended = attended.reshape(block_len, model_width).astype(jnp.bfloat16)
    activated = gelu_tanh(pre_act).astype(jnp.bfloat16)
    attn_branch = jnp.dot(attended, w_out, preferred_element_type=jnp.float32)
    mlp_branch = jnp.dot(activated, w_mlp, preferred_element_type=jnp.float32)
    output = inputs + attn_branch + mlp_branch + bias_out.astype(jnp.float32)
    saved_state = (
        standard,
        inverse_std,
        normed,
        query_rows,
        key_rows,
        value_rows,
        pre_act,
        log_total,
        attended,
        activated,
        same_image,
    )
    return (saved_state, output.astype(jnp.bfloat16))


def backward_block(saved_state, block_cot, gathered):
    (
        standard,
        inverse_std,
        normed,
        query_rows,
        key_rows,
        value_rows,
        pre_act,
        log_total,
        attended,
        activated,
        same_image,
    ) = saved_state
    w_joined, w_out, w_mlp, norm_gain, bias_attn, bias_mlp, bias_out = gathered
    block_len, head_count, head_size = query_rows.shape
    model_width = head_count * head_size
    score_scale = head_size ** (-0.5)
    upstream = block_cot.astype(jnp.float32)
    grad_bias_out = jnp.sum(upstream, axis=0)
    grad_mlp = jnp.einsum("tf,td->fd", activated, block_cot, preferred_element_type=jnp.float32)
    d_act = jnp.einsum("td,fd->tf", block_cot, w_mlp, preferred_element_type=jnp.float32)
    gelu_out, gelu_back = jax.vjp(gelu_tanh, pre_act)
    d_pre = gelu_back(d_act)[0]
    grad_out = jnp.einsum("tc,td->cd", attended, block_cot, preferred_element_type=jnp.float32)
    d_att = jnp.einsum("td,cd->tc", block_cot, w_out, preferred_element_type=jnp.float32)
    d_att = d_att.astype(jnp.bfloat16).reshape(block_len, head_count, head_size)
    scores = masked_scores(query_rows, key_rows, same_image, score_scale)
    attn_probs = jnp.exp(scores - log_total)
    probs_low = attn_probs.astype(jnp.bfloat16)
    d_values = jnp.einsum("hqk,qhe->khe", probs_low, d_att, preferred_element_type=jnp.float32)
    d_probs = jnp.einsum("qhe,khe->hqk", d_att, value_rows, preferred_element_type=jnp.float32)
    row_inner = jnp.sum(attn_probs * d_probs, axis=2, keepdims=True)
    d_scores = (attn_probs * (d_probs - row_inner)).astype(jnp.bfloat16)
    d_queries = (
        jnp.einsum("hqk,khe->qhe", d_scores, key_rows, preferred_element_type=jnp.float32)
        * score_scale
    )
    d_keys = (
        jnp.einsum("hqk,qhe->khe", d_scores, query_rows, preferred_element_type=jnp.float32)
        * score_scale
    )
    d_joined = jnp.concatenate(
        [
            d_queries.reshape(block_len, model_width),
            d_keys.reshape(block_len, model_width),
            d_values.reshape(block_len, model_width),
            d_pre,
        ],
        axis=1,
    ).astype(jnp.bfloat16)
    grad_bias_attn = jnp.concatenate(
        [
            jnp.sum(d_joined[:, :model_width], axis=0, dtype=jnp.float32),
            jnp.sum(d_joined[:, 2 * model_width : 3 * model_width], axis=0, dtype=jnp.float32),
        ]
    )
    grad_bias_mlp = jnp.sum(d_joined[:, 3 * model_width :], axis=0, dtype=jnp.float32)
    grad_joined = jnp.einsum("tc,tf->cf", normed, d_joined, preferred_element_type=jnp.float32)
    d_normed = jnp.einsum("tf,cf->tc", d_joined, w_joined, preferred_element_type=jnp.float32)
    grad_gain = jnp.sum(d_normed * standard, axis=0)
    d_standard = d_normed * norm_gain.astype(jnp.float32)
    mean_grad = jnp.mean(d_standard, axis=1, keepdims=True)
    mean_proj = jnp.mean(d_standard * standard, axis=1, keepdims=True)
    input_grad = upstream + inverse_std * (d_standard - mean_grad - standard * mean_proj)
    grad_terms = (
        grad_joined,
        grad_out,
        grad_mlp,
        grad_gain,
        grad_bias_attn,
        grad_bias_mlp,
        grad_bias_out,
    )
    return (grad_terms, input_grad.astype(jnp.bfloat16))


def body(
    tokens, image_ids, cotangent, w_joined, w_out, w_mlp, norm_gain, bias_attn, bias_mlp, bias_out
):
    micro_count = tokens.shape[0]
    outputs = []
    input_grads = []
    grad_total = None
    for micro_index in range(micro_count):
        forward_weights = (
            lax.all_gather(w_joined, "wide", axis=0, tiled=True),
            lax.all_gather(w_out, "wide", axis=0, tiled=True),
            lax.all_gather(w_mlp, "wide", axis=0, tiled=True),
            lax.all_gather(norm_gain, "wide", axis=0, tiled=True),
            lax.all_gather(bias_attn, "wide", axis=0, tiled=True),
            lax.all_gather(bias_mlp, "wide", axis=0, tiled=True),
            lax.all_gather(bias_out, "wide", axis=0, tiled=True),
        )
        saved_state, output = forward_block(
            tokens[micro_index], image_ids[micro_index], forward_weights
        )
        backward_weights = (
            lax.all_gather(w_joined, "wide", axis=0, tiled=True),
            lax.all_gather(w_out, "wide", axis=0, tiled=True),
            lax.all_gather(w_mlp, "wide", axis=0, tiled=True),
            lax.all_gather(norm_gain, "wide", axis=0, tiled=True),
            lax.all_gather(bias_attn, "wide", axis=0, tiled=True),
            lax.all_gather(bias_mlp, "wide", axis=0, tiled=True),
            lax.all_gather(bias_out, "wide", axis=0, tiled=True),
        )
        grad_terms, input_grad = backward_block(
            saved_state, cotangent[micro_index], backward_weights
        )
        if grad_total is None:
            grad_total = grad_terms
        else:
            grad_total = jax.tree.map(jnp.add, grad_total, grad_terms)
        outputs.append(output)
        input_grads.append(input_grad)
    grad_total = (
        lax.psum_scatter(grad_total[0], "wide", scatter_dimension=0, tiled=True),
        lax.psum_scatter(grad_total[1], "wide", scatter_dimension=0, tiled=True),
        lax.psum_scatter(grad_total[2], "wide", scatter_dimension=0, tiled=True),
        lax.psum_scatter(grad_total[3], "wide", scatter_dimension=0, tiled=True),
        lax.psum_scatter(grad_total[4], "wide", scatter_dimension=0, tiled=True),
        lax.psum_scatter(grad_total[5], "wide", scatter_dimension=0, tiled=True),
        lax.psum_scatter(grad_total[6], "wide", scatter_dimension=0, tiled=True),
    )
    summed = lax.psum(
        (
            grad_total[0],
            grad_total[1],
            grad_total[2],
            grad_total[3],
            grad_total[4],
            grad_total[5],
            grad_total[6],
        ),
        "narrow",
    )
    return (
        jnp.stack(outputs),
        jnp.stack(input_grads),
        summed[0],
        summed[1],
        summed[2],
        summed[3],
        summed[4],
        summed[5],
        summed[6],
    )


def solution(mesh):
    placed = (
        P(None, ("narrow", "wide"), None),
        P(None, ("narrow", "wide")),
        P(None, ("narrow", "wide"), None),
        P("wide", None),
        P("wide", None),
        P("wide", None),
        P("wide"),
        P("wide"),
        P("wide"),
        P("wide"),
    )
    return jax.shard_map(
        body,
        mesh=mesh,
        in_specs=placed,
        out_specs=(
            P(None, ("narrow", "wide"), None),
            P(None, ("narrow", "wide"), None),
            P("wide", None),
            P("wide", None),
            P("wide", None),
            P("wide"),
            P("wide"),
            P("wide"),
            P("wide"),
        ),
        check_vma=False,
    )
```

profile of v0, /device:TPU:0, one launch (start us, length us, event | category | flops | bytes accessed | tf_op | source)
XLA Modules:
  0.0 634.5 jit_solution(8152209839163728400)
XLA Ops:
  20.6 63.7 %all-reduce.11 = (bf16[3072]{0:T(1024)(128)(2,1)S(1)}, bf16[1536]{0:T(1024)(128)(2,1)S(1)}, bf16[768]{0:T(1024)(128)(2,1)S(1)}, bf16[768]{0:T(1024)(128)(2,1)}) all-reduce(bf16[3072]{0:T(1024)(128)(2,1)S(1)} %dynamic-update-slice.2, bf16[1536]{0:T(1024)(128)(2,1)S(1)} %dynamic-update-slice.1, ...), channel_id=1, replica_groups=mesh['narrow'=2,'wide'=16] {'wide'}, use_global_device_ids=true, to_apply=%add.2 | all-reduce | flops 6144 | bytes 24576
  85.5 2.9 convolution_convert_fusion
  89.6 37.3 %all-gather.4.cloned.1.call-done = bf16[768,5376]{1,0:T(8,128)(2,1)} async-done(((bf16[48,5376]{1,0:T(8,128)(2,1)}), bf16[768,5376]{1,0:T(8,128)(2,1)}) %all-gather.4.cloned.1.call-update) | async-done | bytes 8257552 | tf_op jit(solution)/shard_map/all_gather | solution.py:165
  127.0 10.7 %fusion.132 = (bf16[512,5376]{1,0:T(8,128)(2,1)S(1)}, f32[512,5376]{1,0:T(8,128)}) fusion(f32[5376]{0:T(1024)S(1)} %maximum_convert_fusion, bf16[768,5376]{1,0:T(8,128)(2,1)} %all-gather.4.cloned.1.call-done, f32[512]{0:T(512)S(1)} %add_rsqrt_fusion, f32[512]{0:T(512)S(1)} %get-tuple-element.71, f32[768]{0:T(1024)S(1)} %convert_element_type.130, ...), kind=kOutput, calls=%fused_computation.179 | convolution fusion | flops 4235329536 | bytes 25591808 | tf_op jit(solution)/shard_map/dot_general | solution.py:44
  142.9 11.1 %fusion.133 = (bf16[512,5376]{1,0:T(8,128)(2,1)S(1)}, f32[512,5376]{1,0:T(8,128)}) fusion(f32[5376]{0:T(1024)S(1)} %maximum_convert_fusion, bf16[768,5376]{1,0:T(8,128)(2,1)} %all-gather.4.cloned.1.call-done, f32[768]{0:T(1024)S(1)} %convert_element_type.130, f32[512]{0:T(512)S(1)} %add_rsqrt_fusion.1, f32[512]{0:T(512)S(1)} %get-tuple-element.72, ...), kind=kOutput, calls=%fused_computation.180 | convolution fusion | flops 4235329536 | bytes 25591808 | tf_op jit(solution)/shard_map/dot_general | solution.py:44
  166.0 5.0 fusion.73
  175.3 3.7 fusion.1
  179.9 4.9 fusion.72
  188.0 3.2 convolution_convert_fusion.1
  194.3 9.1 %fusion.69 = bf16[12,64,512]{2,1,0:T(8,128)(2,1)} fusion(bf16[512,12,64]{0,2,1:T(8,128)(2,1)} %bitcast.222, f32[12,512]{1,0:T(8,128)S(1)} %log_add_fusion, f32[12,512,512]{1,2,0:T(8,128)} %copy-done.1, pred[512,512]{0,1:T(8,128)(4,1)} %broadcast_compare_fusion), kind=kOutput, calls=%fused_computation.114 | convolution fusion | flops 415629312 | bytes 14442496 | tf_op jit(solution)/shard_map/hqk,qhe->khe/dot_general | solution.py:109
  205.8 6.6 %fusion.88 = f32[3072,768]{1,0:T(8,128)S(1)} fusion(bf16[2,512,768]{2,1,0:T(8,128)(2,1)} %param.12, f32[512,5376]{1,0:T(8,128)} %get-tuple-element.59), kind=kOutput, calls=%fused_computation.131 | convolution fusion | flops 2430074880 | bytes 16515072 | tf_op jit(solution)/shard_map/tf,td->fd/dot_general | solution.py:99
  212.4 10.0 %convolution_add_fusion.3 = f32[3072,768]{1,0:T(8,128)} fusion(f32[3072,768]{1,0:T(8,128)S(1)} %fusion.88, bf16[2,512,768]{2,1,0:T(8,128)(2,1)S(1)} %copy-done.11, f32[512,5376]{1,0:T(8,128)} %get-tuple-element.55), kind=kOutput, calls=%fused_computation.53 | convolution fusion | flops 2432434176 | bytes 25952256 | tf_op jit(solution)/shard_map/tf,td->fd/dot_general | solution.py:99
  222.5 9.6 %multiply_reduce_fusion = (f32[12,512]{1,0:T(8,128)S(1)}, f32[12,512,512]{1,2,0:T(8,128)S(1)}) fusion(f32[12,512]{1,0:T(8,128)S(1)} %log_add_fusion, f32[12,512,512]{1,2,0:T(8,128)} %copy-done.1, pred[512,512]{0,1:T(8,128)(4,1)} %broadcast_compare_fusion, bf16[512,12,64]{0,2,1:T(8,128)(2,1)} %bitcast.223, bf16[512,12,64]{0,2,1:T(8,128)(2,1)} %bitcast.227), kind=kOutput, calls=%fused_computation.1 | convolution fusion | flops 418375680 | bytes 27049984 | tf_op jit(solution)/shard_map/qhe,khe->hqk/dot_general | solution.py:110
  232.1 7.4 %multiply_convert_fusion = bf16[12,512,512]{1,2,0:T(8,128)(2,1)S(1)} fusion(f32[12,512,512]{1,2,0:T(8,128)S(1)} %get-tuple-element.65, f32[12,512]{1,0:T(8,128)S(1)} %get-tuple-element.64, f32[12,512]{1,0:T(8,128)S(1)} %log_add_fusion, f32[12,512,512]{1,2,0:T(8,128)} %copy-done.1, pred[512,512]{0,1:T(8,128)(4,1)S(1)} %copy-done.8), kind=kLoop, calls=%fused_computation | loop fusion | flops 18874368 | bytes 31768576 | tf_op jit(solution)/shard_map/convert_element_type | solution.py:112
  242.1 2.9 multiply_convert_fusion.2
  247.3 3.9 multiply_convert_fusion.3
  252.5 8.9 %fusion.66 = bf16[12,64,512]{2,1,0:T(8,128)(2,1)} fusion(bf16[512,12,64]{0,2,1:T(8,128)(2,1)} %bitcast.228, f32[12,512]{1,0:T(8,128)S(1)} %log_add_fusion.1, f32[12,512,512]{1,2,0:T(8,128)} %copy-done, pred[512,512]{0,1:T(8,128)(4,1)S(1)} %broadcast_compare_fusion.1), kind=kOutput, calls=%fused_computation.113 | convolution fusion | flops 415629312 | bytes 14442496 | tf_op jit(solution)/shard_map/hqk,qhe->khe/dot_general | solution.py:109
  263.7 8.5 %multiply_reduce_fusion.1 = (f32[12,512]{1,0:T(8,128)S(1)}, f32[12,512,512]{1,2,0:T(8,128)S(1)}) fusion(f32[12,512]{1,0:T(8,128)S(1)} %log_add_fusion.1, f32[12,512,512]{1,2,0:T(8,128)} %copy-done, pred[512,512]{0,1:T(8,128)(4,1)S(1)} %broadcast_compare_fusion.1, bf16[512,12,64]{0,2,1:T(8,128)(2,1)} %bitcast.229, bf16[512,12,64]{0,2,1:T(8,128)(2,1)S(1)} %bitcast.225), kind=kOutput, calls=%fused_computation.4 | convolution fusion | flops 418375680 | bytes 27049984 | tf_op jit(solution)/shard_map/qhe,khe->hqk/dot_general | solution.py:110
  272.2 7.7 %multiply_convert_fusion.1 = bf16[12,512,512]{1,2,0:T(8,128)(2,1)S(1)} fusion(f32[12,512,512]{1,2,0:T(8,128)S(1)} %get-tuple-element.63, f32[12,512]{1,0:T(8,128)S(1)} %get-tuple-element.62, f32[12,512]{1,0:T(8,128)S(1)} %log_add_fusion.1, f32[12,512,512]{1,2,0:T(8,128)} %copy-done, pred[512,512]{0,1:T(8,128)(4,1)S(1)} %broadcast_compare_fusion.1), kind=kLoop, calls=%fused_computation.3 | loop fusion | flops 18874368 | bytes 31768576 | tf_op jit(solution)/shard_map/convert_element_type | solution.py:112
  280.0 2.7 copy-done.3
  285.8 4.0 multiply_convert_fusion.5
  291.0 10.1 %convert_reduce_fusion.1 = (f32[3072]{0:T(1024)S(1)}, bf16[512,3072]{1,0:T(8,128)(2,1)S(1)}) fusion(f32[512,5376]{1,0:T(8,128)} %get-tuple-element.59, bf16[3072,768]{1,0:T(8,128)(2,1)} %all-gather.8.cloned.1.call-done, bf16[2,512,768]{2,1,0:T(8,128)(2,1)} %param.12), kind=kOutput, calls=%fused_computation.42 | convolution fusion | flops 2456810496 | bytes 14954496 | tf_op jit(solution)/shard_map/td,fd->tf/dot_general | solution.py:100
  301.2 9.0 %fusion.77 = f32[768,5376]{1,0:T(8,128)} fusion(bf16[512,3072]{1,0:T(8,128)(2,1)S(1)} %get-tuple-element.68, bf16[512,768]{1,0:T(8,128)(2,1)S(1)} %copy-done.21, bf16[512,768]{1,0:T(8,128)(2,1)S(1)} %copy-done.23, bf16[512,768]{1,0:T(8,128)(2,1)S(1)} %copy-done.25, f32[768]{0:T(1024)S(1)} %copy-done.18, f32[512]{0:T(512)S(1)} %copy-done.38, ...), kind=kOutput, calls=%fused_computation.122 | convolution fusion | flops 4251844608 | bytes 22814720 | tf_op jit(solution)/shard_map/tc,tf->cf/dot_general | solution.py:137
  310.2 10.2 %convert_reduce_fusion = (f32[3072]{0:T(1024)S(1)}, bf16[512,3072]{1,0:T(8,128)(2,1)}) fusion(f32[512,5376]{1,0:T(8,128)} %get-tuple-element.55, bf16[3072,768]{1,0:T(8,128)(2,1)S(1)} %copy-done.40, bf16[2,512,768]{2,1,0:T(8,128)(2,1)S(1)} %copy-done.12), kind=kOutput, calls=%fused_computation.41 | convolution fusion | flops 2456810496 | bytes 14954496 | tf_op jit(solution)/shard_map/td,fd->tf/dot_general | solution.py:100
  320.4 13.5 %convolution_add_fusion = f32[768,5376]{1,0:T(8,128)} fusion(f32[768,5376]{1,0:T(8,128)} %fusion.77, bf16[512,3072]{1,0:T(8,128)(2,1)} %get-tuple-element.70, bf16[512,768]{1,0:T(8,128)(2,1)S(1)} %copy-done.15, bf16[512,768]{1,0:T(8,128)(2,1)S(1)} %copy-done.16, bf16[512,768]{1,0:T(8,128)(2,1)} %copy.90, f32[512]{0:T(512)S(1)} %copy-done.33, ...), kind=kOutput, calls=%fused_computation.14 | convolution fusion | flops 4255973376 | bytes 39329792 | tf_op jit(solution)/shard_map/tc,tf->cf/dot_general | solution.py:137
  339.0 9.6 %fusion.76 = f32[512,768]{1,0:T(8,128)S(1)} fusion(bf16[768,5376]{1,0:T(8,128)(2,1)} %all-gather.4.cloned.1.call-done, bf16[512,3072]{1,0:T(8,128)(2,1)} %get-tuple-element.70, bf16[512,768]{1,0:T(8,128)(2,1)} %copy.92, bf16[512,768]{1,0:T(8,128)(2,1)} %copy.91, bf16[512,768]{1,0:T(8,128)(2,1)} %copy.90), kind=kOutput, calls=%fused_computation.121 | convolution fusion | flops 4249878528 | bytes 15335424 | tf_op jit(solution)/shard_map/tf,cf->tc/dot_general | solution.py:138
  348.6 9.2 %fusion.56 = (f32[768]{0:T(1024)S(1)}, f32[512]{0:T(512)S(1)}, f32[512]{0:T(512)S(1)}, f32[768]{0:T(1024)S(1)}, f32[512]{0:T(512)S(1)}, /*index=5*/f32[512]{0:T(512)S(1)}, f32[512,768]{1,0:T(8,128)S(1)}) fusion(f32[512]{0:T(512)S(1)} %copy-done.38, f32[512]{0:T(512)S(1)} %copy-done.36, bf16[2,512,768]{2,1,0:T(8,128)(2,1)S(1)} %copy-done.5, ...), kind=kOutput, calls=%fused_computation.91 | convolution fusion | flops 4256952832 | bytes 18506752 | tf_op jit(solution)/shard_map/tf,cf->tc/dot_general | solution.py:138
  357.9 6.1 fusion.125
  367.4 177.4 %reduce-scatter.4.cloned.1.call-done = f32[48,5376]{1,0:T(8,128)} async-done(((f32[768,5376]{1,0:T(8,128)}), f32[48,5376]{1,0:T(8,128)}) %reduce-scatter.4.cloned.1.call-update) | async-done | bytes 1032208 | tf_op jit(solution)/shard_map/reduce_scatter | solution.py:195
  544.9 59.6 %all-reduce.8 = (f32[768]{0:T(1024)S(1)}, f32[1536]{0:T(1024)S(1)}, f32[3072]{0:T(1024)S(1)}, f32[768]{0:T(1024)S(1)}) all-reduce(f32[768]{0:T(1024)S(1)} %add.168, f32[1536]{0:T(1024)S(1)} %maximum_add_fusion, f32[3072]{0:T(1024)S(1)} %add.170, f32[768]{0:T(1024)S(1)} %add.171), channel_id=5, replica_groups=mesh['narrow'=2,'wide'=16] {'wide'}, use_global_device_ids=true, to_apply=%region_22.23.clone | all-reduce | flops 6144 | bytes 49152
  604.8 5.5 all-reduce.9
  610.2 7.5 %fusion.122 = f32[512,768]{1,0:T(8,128)S(1)} fusion(bf16[3072,768]{1,0:T(8,128)(2,1)} %all-gather.8.cloned.1.call-done, f32[512,5376]{1,0:T(8,128)} %get-tuple-element.59), kind=kOutput, calls=%fused_computation.172 | convolution fusion | flops 2430074880 | bytes 12582912 | tf_op jit(solution)/shard_map/dot_general | solution.py:61
  (181 shorter events, 73.7 us)
Async XLA Ops:
  7.2 119.8 %copy-start.4 = (bf16[2,512,768]{2,1,0:T(8,128)(2,1)S(1)}, bf16[2,512,768]{2,1,0:T(8,128)(2,1)}, u32[]{:S(2)}) copy-start(bf16[2,512,768]{2,1,0:T(8,128)(2,1)} %param.10) | copy-start | bytes 4718596
  7.2 78.3 %all-gather.6.cloned.1.call-start = ((), (), s32[]{:S(2)}) async-start(), calls=%async_computation.4 | async-start | bytes 1253376 | tf_op jit(solution)/shard_map/all_gather | solution.py:166
  7.9 119.1 %all-gather.4.cloned.1.call-start = ((), (), s32[]{:S(2)}) async-start(), calls=%async_computation.3 | async-start | bytes 8773632 | tf_op jit(solution)/shard_map/all_gather | solution.py:165
  8.7 282.3 %all-gather.8.cloned.1.call-start = ((), (), s32[]{:S(2)}) async-start(), calls=%async_computation.5 | async-start | bytes 5013504 | tf_op jit(solution)/shard_map/all_gather | solution.py:167
  9.4 358.0 %reduce-scatter.6.cloned.1.call-start = ((), (), s32[]{:S(2)}) async-start(), calls=%async_computation.7 | async-start | bytes 2506752 | tf_op jit(solution)/shard_map/reduce_scatter | solution.py:196
  15.2 122.5 %copy-start.30 = (f32[512]{0:T(512)}, f32[512]{0:T(512)S(1)}, u32[]{:S(2)}) copy-start(f32[512]{0:T(512)S(1)} %get-tuple-element.71) | copy-start | bytes 6148
  15.2 127.8 %copy-start.35 = (f32[512]{0:T(512)}, f32[512]{0:T(512)S(1)}, u32[]{:S(2)}) copy-start(f32[512]{0:T(512)S(1)} %get-tuple-element.72) | copy-start | bytes 6148
  17.1 125.8 %copy-start.37 = (f32[512]{0:T(512)}, f32[512]{0:T(512)S(1)}, u32[]{:S(2)}) copy-start(f32[512]{0:T(512)S(1)} %add_rsqrt_fusion.1) | copy-start | bytes 6148
  17.2 120.5 %copy-start.32 = (f32[512]{0:T(512)}, f32[512]{0:T(512)S(1)}, u32[]{:S(2)}) copy-start(f32[512]{0:T(512)S(1)} %add_rsqrt_fusion) | copy-start | bytes 6148
  84.3 58.6 %copy-start.17 = (f32[768]{0:T(1024)}, f32[768]{0:T(1024)S(1)}, u32[]{:S(2)}) copy-start(f32[768]{0:T(1024)S(1)} %convert_element_type.130) | copy-start | bytes 9220
  187.9 179.5 %reduce-scatter.8.cloned.1.call-start = ((), (), s32[]{:S(2)}) async-start(), calls=%async_computation.8 | async-start | bytes 10027008 | tf_op jit(solution)/shard_map/reduce_scatter | solution.py:197
  222.4 322.4 %reduce-scatter.4.cloned.1.call-start = ((), (), s32[]{:S(2)}) async-start(), calls=%async_computation.6 | async-start | bytes 17547264 | tf_op jit(solution)/shard_map/reduce_scatter | solution.py:195
  222.5 9.6 %copy-start.8 = (pred[512,512]{0,1:T(8,128)(4,1)S(1)}, pred[512,512]{0,1:T(8,128)(4,1)}, u32[]{:S(2)}) copy-start(pred[512,512]{0,1:T(8,128)(4,1)} %broadcast_compare_fusion) | copy-start | bytes 786436
  252.5 11.3 %copy-start.14 = (bf16[512,768]{0,1:T(8,128)(2,1)S(1)}, bf16[512,768]{0,1:T(8,128)(2,1)}, u32[]{:S(2)}) copy-start(bf16[512,768]{0,1:T(8,128)(2,1)} %copy.71) | copy-start | bytes 2359300
  290.9 10.2 %copy-start.5 = (bf16[2,512,768]{2,1,0:T(8,128)(2,1)S(1)}, bf16[2,512,768]{2,1,0:T(8,128)(2,1)}, u32[]{:S(2)}) copy-start(bf16[2,512,768]{2,1,0:T(8,128)(2,1)} %param.10) | copy-start | bytes 4718596
  290.9 10.2 %copy-start.18 = (f32[768]{0:T(1024)S(1)}, f32[768]{0:T(1024)}, u32[]{:S(2)}) copy-start(f32[768]{0:T(1024)} %copy-done.17) | copy-start | bytes 9220
  290.9 10.2 %copy-start.36 = (f32[512]{0:T(512)S(1)}, f32[512]{0:T(512)}, u32[]{:S(2)}) copy-start(f32[512]{0:T(512)} %copy-done.35) | copy-start | bytes 6148
  290.9 10.2 %copy-start.38 = (f32[512]{0:T(512)S(1)}, f32[512]{0:T(512)}, u32[]{:S(2)}) copy-start(f32[512]{0:T(512)} %copy-done.37) | copy-start | bytes 6148
  290.9 10.2 %copy-start.21 = (bf16[512,768]{1,0:T(8,128)(2,1)S(1)}, bf16[512,768]{1,0:T(8,128)(2,1)}, u32[]{:S(2)}) copy-start(bf16[512,768]{1,0:T(8,128)(2,1)} %copy.85) | copy-start | bytes 2359300
  291.0 10.2 %copy-start.23 = (bf16[512,768]{1,0:T(8,128)(2,1)S(1)}, bf16[512,768]{1,0:T(8,128)(2,1)}, u32[]{:S(2)}) copy-start(bf16[512,768]{1,0:T(8,128)(2,1)} %copy.84) | copy-start | bytes 2359300
  291.0 10.2 %copy-start.25 = (bf16[512,768]{1,0:T(8,128)(2,1)S(1)}, bf16[512,768]{1,0:T(8,128)(2,1)}, u32[]{:S(2)}) copy-start(bf16[512,768]{1,0:T(8,128)(2,1)} %copy.83) | copy-start | bytes 2359300
  301.1 9.1 %copy-start.43 = (bf16[512,3072]{1,0:T(8,128)(2,1)}, bf16[512,3072]{1,0:T(8,128)(2,1)S(1)}, u32[]{:S(2)}) copy-start(bf16[512,3072]{1,0:T(8,128)(2,1)S(1)} %get-tuple-element.68) | copy-start | bytes 9437188
  310.2 10.2 %copy-start.15 = (bf16[512,768]{1,0:T(8,128)(2,1)S(1)}, bf16[512,768]{1,0:T(8,128)(2,1)}, u32[]{:S(2)}) copy-start(bf16[512,768]{1,0:T(8,128)(2,1)} %copy.92) | copy-start | bytes 2359300
  310.2 10.2 %copy-start.16 = (bf16[512,768]{1,0:T(8,128)(2,1)S(1)}, bf16[512,768]{1,0:T(8,128)(2,1)}, u32[]{:S(2)}) copy-start(bf16[512,768]{1,0:T(8,128)(2,1)} %copy.91) | copy-start | bytes 2359300
  310.2 10.2 %copy-start.31 = (f32[512]{0:T(512)S(1)}, f32[512]{0:T(512)}, u32[]{:S(2)}) copy-start(f32[512]{0:T(512)} %copy-done.30) | copy-start | bytes 6148
  310.2 10.2 %copy-start.33 = (f32[512]{0:T(512)S(1)}, f32[512]{0:T(512)}, u32[]{:S(2)}) copy-start(f32[512]{0:T(512)} %copy-done.32) | copy-start | bytes 6148
  333.9 287.6 %all-reduce.14.cloned.1.call-start = ((), (), s32[]{:S(2)}) async-start(), calls=%async_computation.9 | async-start | bytes 3538944 | tf_op jit(solution)/shard_map/psum | solution.py:203
  338.9 9.6 %copy-start.22 = (bf16[512,768]{1,0:T(8,128)(2,1)S(1)}, bf16[512,768]{1,0:T(8,128)(2,1)}, u32[]{:S(2)}) copy-start(bf16[512,768]{1,0:T(8,128)(2,1)} %copy.85) | copy-start | bytes 2359300
  338.9 9.6 %copy-start.24 = (bf16[512,768]{1,0:T(8,128)(2,1)S(1)}, bf16[512,768]{1,0:T(8,128)(2,1)}, u32[]{:S(2)}) copy-start(bf16[512,768]{1,0:T(8,128)(2,1)} %copy.84) | copy-start | bytes 2359300
  339.0 9.6 %copy-start.26 = (bf16[512,768]{1,0:T(8,128)(2,1)S(1)}, bf16[512,768]{1,0:T(8,128)(2,1)}, u32[]{:S(2)}) copy-start(bf16[512,768]{1,0:T(8,128)(2,1)} %copy.83) | copy-start | bytes 2359300
  339.0 18.8 %slice-start = ((s8[4718592]{0:T(1024)(128)(4,1)}), s8[4194304]{0:T(1024)(128)(4,1)S(1)}, s32[]{:S(2)}) async-start(s8[4718592]{0:T(1024)(128)(4,1)} %bitcast.240), calls=%async_computation.10 | async-start | bytes 8388608
  348.6 9.2 %slice-start.1 = ((s8[4718592]{0:T(1024)(128)(4,1)}), s8[524288]{0:T(1024)(128)(4,1)S(1)}, s32[]{:S(2)}) async-start(s8[4718592]{0:T(1024)(128)(4,1)} %bitcast.240), calls=%async_computation.11 | async-start | bytes 1048576
  (21 other events, 106.2 us)
Sparse Core Ops, SparseCore 0:
  10.3 41.2 all-gather.5
  53.9 73.0 all-gather.3
  129.3 51.4 all-gather.7
  188.0 61.4 reduce-scatter.5
  254.0 110.3 reduce-scatter.7
  368.5 176.3 reduce-scatter.3
  547.4 55.1 all-reduce.13
where the time goes:
time: 643 us; the launch traced here: 635 us
  waiting for transfers between devices  217 us (34%)
  matrix products  190 us (30%)
  blocking collectives  129 us (20%)
  local copies, waits for them, and re-layouts  45.4 us (7%)
  other arithmetic  34.3 us (5%)
  between operations  19.3 us (3%)
    reduce_scatter x1, waiting for transfers between devices, body(): lax.psum_scatter(grad_total[0], 'wide', scatter_dimension=0, tiled=True)  177 us
    unnamed x2, blocking collectives  123 us
    all_gather x1, waiting for transfers between devices, body(): lax.all_gather(w_joined, 'wide', axis=0, tiled=True)  37.3 us
    dot_general x2, matrix products, backward_block(): jnp.einsum('tc,tf->cf', normed, d_joined, preferred_element_type=jnp.floa...  22.5 us
    dot_general x2, matrix products, forward_block(): jnp.dot(normed, w_joined, preferred_element_type=jnp.float32) + bias_full  21.8 us
    dot_general x2, matrix products, backward_block(): jnp.einsum('td,fd->tf', block_cot, w_mlp, preferred_element_type=jnp.floa...  20.2 us
    unnamed x109, local copies, waits for them, and re-layouts  20.1 us
    dot_general x2, matrix products, backward_block(): jnp.einsum('tf,cf->tc', d_joined, w_joined, preferred_element_type=jnp.fl...  18.7 us
  transfers between devices with their start and end apart: 7, of which 2 were waited for; matrix products, arithmetic and copies ran while one was open for 40% of the time, Pallas kernels for 0%

commit v1 on v0

--- a/solution.py
+++ b/solution.py
@@ -6,6 +6,27 @@
 HEADS = 12
 norm_eps = 1e-06
 masked_score = -1e30
+
+
+def joined_along(parts, dim):
+    parts = jnp.moveaxis(parts, 0, dim)
+    lengths = parts.shape
+    return parts.reshape(*lengths[:dim], lengths[dim] * lengths[dim + 1], *lengths[dim + 2 :])
+
+
+def grow_blocks(shard, axis):
+    size, index = (lax.axis_size(axis), lax.axis_index(axis))
+    tiles, bit = (shard[None], 1)
+    while bit < size:
+        other = lax.ppermute(tiles, axis, [(i, i ^ bit) for i in range(size)])
+        low = index & bit == 0
+        tiles = jnp.concatenate([jnp.where(low, tiles, other), jnp.where(low, other, tiles)])
+        bit *= 2
+    return tiles
+
+
+def doubled_up(value, axis, dim):
+    return joined_along(grow_blocks(value, axis), dim)
 
 
 def gelu_tanh(inputs):
@@ -162,7 +183,7 @@
     grad_total = None
     for micro_index in range(micro_count):
         forward_weights = (
-            lax.all_gather(w_joined, "wide", axis=0, tiled=True),
+            doubled_up(w_joined, "wide", 0),
             lax.all_gather(w_out, "wide", axis=0, tiled=True),
             lax.all_gather(w_mlp, "wide", axis=0, tiled=True),
             lax.all_gather(norm_gain, "wide", axis=0, tiled=True),

time: 643 us -> 924 us (1.44)
  blocking collectives: 129 us -> 326 us
  waiting for transfers between devices: 217 us -> 286 us
  other arithmetic: 34.3 us -> 52.7 us
    unnamed x2, blocking collectives: 123 us -> 320 us
    ppermute x0 -> x4, waiting for transfers between devices: none -> 102 us  [grow_blocks(): other = lax.ppermute(tiles, axis, [(i, i ^ bit) for i in range(size)])]
    all_gather x1, waiting for transfers between devices: 37.3 us -> 0.01 us  [body(): lax.all_gather(w_joined, 'wide', axis=0, tiled=True)]
    concatenate x0 -> x4, other arithmetic: none -> 11.5 us  [grow_blocks(): jnp.concatenate([jnp.where(low, tiles, other), jnp.where(low, other, tile...]
    select_n x0 -> x4, other arithmetic: none -> 9.97 us  [grow_blocks(): jnp.where(low, tiles, other)]
    unnamed x109 -> x133, local copies, waits for them, and re-layouts: 20.1 us -> 19.1 us
  transfers between devices with their start and end apart: 7 -> 11, of which waited for: 2 -> 5; matrix products, arithmetic and copies ran while one was open for 40% -> 29% of each run, Pallas kernels for 0% -> 0%
where the time goes in v1:
time: 924 us; the launch traced here: 920 us
  blocking collectives  326 us (35%)
  waiting for transfers between devices  286 us (31%)
  matrix products  185 us (20%)
  other arithmetic  52.7 us (6%)
  local copies, waits for them, and re-layouts  43.9 us (5%)
  between operations  19.2 us (2%)
    unnamed x2, blocking collectives  320 us
    reduce_scatter x1, waiting for transfers between devices, body(): lax.psum_scatter(grad_total[0], 'wide', scatter_dimension=0, tiled=True)  180 us
    ppermute x4, waiting for transfers between devices, grow_blocks(): other = lax.ppermute(tiles, axis, [(i, i ^ bit) for i in range(size)])  102 us
    dot_general x2, matrix products, backward_block(): jnp.einsum('tc,tf->cf', normed, d_joined, preferred_element_type=jnp.floa...  22 us
    dot_general x2, matrix products, forward_block(): jnp.dot(normed, w_joined, preferred_element_type=jnp.float32) + bias_full  21.8 us
    dot_general x2, matrix products, backward_block(): jnp.einsum('td,fd->tf', block_cot, w_mlp, preferred_element_type=jnp.floa...  20.4 us
    dot_general x2, matrix products, backward_block(): jnp.einsum('tf,cf->tc', d_joined, w_joined, preferred_element_type=jnp.fl...  19.2 us
    unnamed x133, local copies, waits for them, and re-layouts  19.1 us
  transfers between devices with their start and end apart: 11, of which 5 were waited for; matrix products, arithmetic and copies ran while one was open for 29% of the time, Pallas kernels for 0%

profile of v1, /device:TPU:0, one launch (start us, length us, event | category | flops | bytes accessed | tf_op | source)
XLA Modules:
  0.0 919.8 jit_solution(5900649157938397362)
XLA Ops:
  13.7 23.9 %collective-permute-done.1 = bf16[2,48,5376]{2,1,0:T(8,128)(2,1)} collective-permute-done((bf16[2,48,5376]{2,1,0:T(8,128)(2,1)S(1)}, bf16[2,48,5376]{2,1,0:T(8,128)(2,1)}, u32[]{:S(2)}, u32[]{:S(2)}) %collective-permute-start.1) | collective-permute-done | bytes 1032224 | tf_op jit(solution)/shard_map/ppermute | solution.py:21
  42.3 76.2 %collective-permute-done.2 = bf16[4,48,5376]{2,1,0:T(8,128)(2,1)} collective-permute-done((bf16[4,48,5376]{2,1,0:T(8,128)(2,1)}, bf16[4,48,5376]{2,1,0:T(8,128)(2,1)}, u32[]{:S(2)}, u32[]{:S(2)}) %collective-permute-start.2) | collective-permute-done | bytes 2064416 | tf_op jit(solution)/shard_map/ppermute | solution.py:21
  129.1 260.5 %all-reduce.11 = (bf16[3072]{0:T(1024)(128)(2,1)S(1)}, bf16[1536]{0:T(1024)(128)(2,1)S(1)}, bf16[768]{0:T(1024)(128)(2,1)S(1)}, bf16[768]{0:T(1024)(128)(2,1)}) all-reduce(bf16[3072]{0:T(1024)(128)(2,1)S(1)} %dynamic-update-slice.2, bf16[1536]{0:T(1024)(128)(2,1)S(1)} %dynamic-update-slice.1, ...), channel_id=1, replica_groups=mesh['narrow'=2,'wide'=16] {'wide'}, use_global_device_ids=true, to_apply=%add.2 | all-reduce | flops 6144 | bytes 24576
  397.2 5.7 broadcast_select_fusion.1
  402.8 7.4 pad_maximum_fusion
  410.2 10.6 %fusion.156 = (bf16[512,5376]{1,0:T(8,128)(2,1)S(1)}, f32[512,5376]{1,0:T(8,128)}) fusion(f32[5376]{0:T(1024)S(1)} %maximum_convert_fusion, bf16[768,5376]{1,0:T(8,128)(2,1)} %bitcast.220, f32[512]{0:T(512)S(1)} %add_rsqrt_fusion, f32[512]{0:T(512)S(1)} %get-tuple-element.79, f32[768]{0:T(1024)S(1)} %convert_element_type.142, ...), kind=kOutput, calls=%fused_computation.217 | convolution fusion | flops 4235329536 | bytes 25591808 | tf_op jit(solution)/shard_map/dot_general | solution.py:65
  426.5 11.2 %fusion.157 = (bf16[512,5376]{1,0:T(8,128)(2,1)S(1)}, f32[512,5376]{1,0:T(8,128)}) fusion(f32[5376]{0:T(1024)S(1)} %maximum_convert_fusion, bf16[768,5376]{1,0:T(8,128)(2,1)} %bitcast.221, f32[768]{0:T(1024)S(1)} %convert_element_type.142, f32[512]{0:T(512)S(1)} %add_rsqrt_fusion.1, f32[512]{0:T(512)S(1)} %get-tuple-element.80, ...), kind=kOutput, calls=%fused_computation.218 | convolution fusion | flops 4235329536 | bytes 25591808 | tf_op jit(solution)/shard_map/dot_general | solution.py:65
  446.0 3.7 fusion
  450.5 5.1 fusion.79
  464.4 3.6 fusion.78
  476.7 9.3 %fusion.72 = bf16[12,64,512]{2,1,0:T(8,128)(2,1)} fusion(bf16[512,12,64]{0,2,1:T(8,128)(2,1)} %bitcast.238, f32[12,512]{1,0:T(8,128)S(1)} %log_add_fusion.1, f32[12,512,512]{1,2,0:T(8,128)} %copy-done.1, pred[512,512]{0,1:T(8,128)(4,1)S(1)} %copy-done.13), kind=kOutput, calls=%fused_computation.128 | convolution fusion | flops 415629312 | bytes 14442496 | tf_op jit(solution)/shard_map/hqk,qhe->khe/dot_general | solution.py:130
  488.4 6.5 fusion.100
  494.9 9.8 %convolution_add_fusion.3 = f32[3072,768]{1,0:T(8,128)} fusion(f32[3072,768]{1,0:T(8,128)S(1)} %fusion.100, bf16[2,512,768]{2,1,0:T(8,128)(2,1)S(1)} %copy-done.17, f32[512,5376]{1,0:T(8,128)} %get-tuple-element.63), kind=kOutput, calls=%fused_computation.54 | convolution fusion | flops 2432434176 | bytes 25952256 | tf_op jit(solution)/shard_map/tf,td->fd/dot_general | solution.py:120
  504.7 9.5 %multiply_reduce_fusion.1 = (f32[12,512]{1,0:T(8,128)S(1)}, f32[12,512,512]{1,2,0:T(8,128)S(1)}) fusion(f32[12,512]{1,0:T(8,128)S(1)} %log_add_fusion.1, f32[12,512,512]{1,2,0:T(8,128)} %copy-done.1, pred[512,512]{0,1:T(8,128)(4,1)S(1)} %copy-done.13, bf16[512,12,64]{0,2,1:T(8,128)(2,1)} %bitcast.239, bf16[512,12,64]{0,2,1:T(8,128)(2,1)} %bitcast.237), kind=kOutput, calls=%fused_computation.4 | convolution fusion | flops 418375680 | bytes 27049984 | tf_op jit(solution)/shard_map/qhe,khe->hqk/dot_general | solution.py:131
  514.2 7.4 multiply_convert_fusion.1
  527.5 4.0 multiply_convert_fusion.5
  532.7 7.3 fusion.75
  542.3 7.6 multiply_reduce_fusion
  550.0 8.1 multiply_convert_fusion
  563.9 3.9 multiply_convert_fusion.3
  570.0 10.3 %convert_reduce_fusion.1 = (f32[3072]{0:T(1024)S(1)}, bf16[512,3072]{1,0:T(8,128)(2,1)S(1)}) fusion(f32[512,5376]{1,0:T(8,128)} %get-tuple-element.67, bf16[3072,768]{1,0:T(8,128)(2,1)} %all-gather.6.cloned.1.call-done, bf16[2,512,768]{2,1,0:T(8,128)(2,1)} %param.12), kind=kOutput, calls=%fused_computation.43 | convolution fusion | flops 2456810496 | bytes 14954496 | tf_op jit(solution)/shard_map/td,fd->tf/dot_general | solution.py:121
  580.3 9.0 fusion.83
  589.4 10.1 %convert_reduce_fusion = (f32[3072]{0:T(1024)S(1)}, bf16[512,3072]{1,0:T(8,128)(2,1)}) fusion(f32[512,5376]{1,0:T(8,128)} %get-tuple-element.63, bf16[3072,768]{1,0:T(8,128)(2,1)S(1)} %copy-done.49, bf16[2,512,768]{2,1,0:T(8,128)(2,1)S(1)} %copy-done.18), kind=kOutput, calls=%fused_computation.42 | convolution fusion | flops 2456810496 | bytes 14954496 | tf_op jit(solution)/shard_map/td,fd->tf/dot_general | solution.py:121
  599.6 12.9 %convolution_add_fusion = f32[768,5376]{1,0:T(8,128)} fusion(f32[768,5376]{1,0:T(8,128)} %fusion.83, bf16[512,3072]{1,0:T(8,128)(2,1)} %get-tuple-element.78, bf16[512,768]{1,0:T(8,128)(2,1)S(1)} %copy-done.23, bf16[512,768]{1,0:T(8,128)(2,1)S(1)} %copy-done.25, bf16[512,768]{1,0:T(8,128)(2,1)S(1)} %copy-done.27, f32[512]{0:T(512)S(1)} %copy-done.41, ...), kind=kOutput, calls=%fused_computation.14 | convolution fusion | flops 4255973376 | bytes 39329792 | tf_op jit(solution)/shard_map/tc,tf->cf/dot_general | solution.py:158
  618.0 7.9 fusion.146
  626.9 6.0 fusion.149
  635.1 9.6 %fusion.82 = f32[512,768]{1,0:T(8,128)} fusion(bf16[768,5376]{1,0:T(8,128)(2,1)} %all-gather.8.cloned.1.call-done, bf16[512,3072]{1,0:T(8,128)(2,1)} %get-tuple-element.78, bf16[512,768]{1,0:T(8,128)(2,1)S(1)} %copy-done.24, bf16[512,768]{1,0:T(8,128)(2,1)S(1)} %copy-done.26, bf16[512,768]{1,0:T(8,128)(2,1)} %copy.90), kind=kOutput, calls=%fused_computation.139 | convolution fusion | flops 4249878528 | bytes 15335424 | tf_op jit(solution)/shard_map/tf,cf->tc/dot_general | solution.py:159
  644.7 3.9 reduce-scatter.8.cloned.1.call-done
  648.6 180.5 %reduce-scatter.4.cloned.1.call-done = f32[48,5376]{1,0:T(8,128)} async-done(((f32[768,5376]{1,0:T(8,128)}), f32[48,5376]{1,0:T(8,128)}) %reduce-scatter.4.cloned.1.call-update) | async-done | bytes 1032208 | tf_op jit(solution)/shard_map/reduce_scatter | solution.py:216
  829.1 9.6 %fusion.50 = (f32[768]{0:T(1024)S(1)}, f32[512]{0:T(512)S(1)}, f32[512]{0:T(512)S(1)}, f32[768]{0:T(1024)S(1)}, f32[512]{0:T(512)S(1)}, /*index=5*/f32[512]{0:T(512)S(1)}, f32[512,768]{1,0:T(8,128)S(1)}) fusion(f32[512]{0:T(512)S(1)} %copy-done.45, f32[512]{0:T(512)S(1)} %copy-done.43, bf16[2,512,768]{2,1,0:T(8,128)(2,1)S(1)} %copy-done.5, ...), kind=kOutput, calls=%fused_computation.94 | convolution fusion | flops 4256952832 | bytes 18506752 | tf_op jit(solution)/shard_map/tf,cf->tc/dot_general | solution.py:159
  840.5 59.5 %all-reduce.8 = (f32[768]{0:T(1024)S(1)}, f32[1536]{0:T(1024)S(1)}, f32[3072]{0:T(1024)S(1)}, f32[768]{0:T(1024)S(1)}) all-reduce(f32[768]{0:T(1024)S(1)} %add.168, f32[1536]{0:T(1024)S(1)} %maximum_add_fusion, f32[3072]{0:T(1024)S(1)} %add.170, f32[768]{0:T(1024)S(1)} %add.171), channel_id=5, replica_groups=mesh['narrow'=2,'wide'=16] {'wide'}, use_global_device_ids=true, to_apply=%region_22.23.clone | all-reduce | flops 6144 | bytes 49152
  900.3 5.5 all-reduce.9
  (221 shorter events, 94.4 us)
Async XLA Ops:
  7.2 384.7 %all-gather.4.cloned.1.call-start = ((), (), s32[]{:S(2)}) async-start(), calls=%async_computation.3 | async-start | bytes 1253376 | tf_op jit(solution)/shard_map/all_gather | solution.py:187
  7.2 2.3 collective-permute-start
  7.9 562.0 %all-gather.6.cloned.1.call-start = ((), (), s32[]{:S(2)}) async-start(), calls=%async_computation.4 | async-start | bytes 5013504 | tf_op jit(solution)/shard_map/all_gather | solution.py:188
  10.7 26.9 %collective-permute-start.1 = (bf16[2,48,5376]{2,1,0:T(8,128)(2,1)S(1)}, bf16[2,48,5376]{2,1,0:T(8,128)(2,1)}, u32[]{:S(2)}, u32[]{:S(2)}) collective-permute-start(bf16[2,48,5376]{2,1,0:T(8,128)(2,1)S(1)} %pad_maximum_fusion.7), channel_id=1, source_target_pairs={{0,2},{1,3},{2,0},{3,1},{4,6},{5,7},{6,4},{7,5},{8,10},{9,11},{10,... | collective-permute-start | bytes 3096584 | tf_op jit(solution)/shard_map/ppermute | solution.py:21
  13.6 621.4 %all-gather.8.cloned.1.call-start = ((), (), s32[]{:S(2)}) async-start(), calls=%async_computation.5 | async-start | bytes 8773632 | tf_op jit(solution)/shard_map/all_gather | solution.py:198
  40.5 78.0 %collective-permute-start.2 = (bf16[4,48,5376]{2,1,0:T(8,128)(2,1)}, bf16[4,48,5376]{2,1,0:T(8,128)(2,1)}, u32[]{:S(2)}, u32[]{:S(2)}) collective-permute-start(bf16[4,48,5376]{2,1,0:T(8,128)(2,1)} %pad_maximum_fusion.4), channel_id=1, source_target_pairs={{0,4},{1,5},{2,6},{3,7},{4,0},{5,1},{6,2},{7,3},{8,12},{9,13},{10,... | collective-permute-start | bytes 6193160 | tf_op jit(solution)/shard_map/ppermute | solution.py:21
  120.5 269.2 %copy-start.4 = (bf16[2,512,768]{2,1,0:T(8,128)(2,1)S(1)}, bf16[2,512,768]{2,1,0:T(8,128)(2,1)}, u32[]{:S(2)}) copy-start(bf16[2,512,768]{2,1,0:T(8,128)(2,1)} %param.10) | copy-start | bytes 4718596
  120.5 270.2 %copy-start.46 = (s32[2,512]{1,0:T(2,128)S(1)}, s32[2,512]{1,0:T(2,128)}, u32[]{:S(2)}) copy-start(s32[2,512]{1,0:T(2,128)} %param.11) | copy-start | bytes 12292
  121.7 270.2 %copy-start.14 = (bf16[2,512,768]{2,1,0:T(8,128)(2,1)S(1)}, bf16[2,512,768]{2,1,0:T(8,128)(2,1)}, u32[]{:S(2)}) copy-start(bf16[2,512,768]{2,1,0:T(8,128)(2,1)} %param.12) | copy-start | bytes 4718596
  124.4 272.8 %collective-permute-start.3 = (bf16[8,48,5376]{2,1,0:T(8,128)(2,1)}, bf16[8,48,5376]{2,1,0:T(8,128)(2,1)}, u32[]{:S(2)}, u32[]{:S(2)}) collective-permute-start(bf16[8,48,5376]{2,1,0:T(8,128)(2,1)} %pad_maximum_fusion.3), channel_id=1, source_target_pairs={{0,8},{1,9},{2,10},{3,11},{4,12},{5,13},{6,14},{7,15},{8,0},{9,1},... | collective-permute-start | bytes 12386312 | tf_op jit(solution)/shard_map/ppermute | solution.py:21
  125.5 519.2 %reduce-scatter.6.cloned.1.call-start = ((), (), s32[]{:S(2)}) async-start(), calls=%async_computation.7 | async-start | bytes 2506752 | tf_op jit(solution)/shard_map/reduce_scatter | solution.py:217
  389.7 36.8 %copy-start.28 = (f32[768]{0:T(1024)}, f32[768]{0:T(1024)S(1)}, u32[]{:S(2)}) copy-start(f32[768]{0:T(1024)S(1)} %convert_element_type.142) | copy-start | bytes 9220
  390.0 20.2 %copy-start.38 = (f32[512]{0:T(512)}, f32[512]{0:T(512)S(1)}, u32[]{:S(2)}) copy-start(f32[512]{0:T(512)S(1)} %get-tuple-element.79) | copy-start | bytes 6148
  390.0 36.4 %copy-start.42 = (f32[512]{0:T(512)}, f32[512]{0:T(512)S(1)}, u32[]{:S(2)}) copy-start(f32[512]{0:T(512)S(1)} %get-tuple-element.80) | copy-start | bytes 6148
  390.6 35.8 %copy-start.44 = (f32[512]{0:T(512)}, f32[512]{0:T(512)S(1)}, u32[]{:S(2)}) copy-start(f32[512]{0:T(512)S(1)} %add_rsqrt_fusion.1) | copy-start | bytes 6148
  390.7 19.6 %copy-start.40 = (f32[512]{0:T(512)}, f32[512]{0:T(512)S(1)}, u32[]{:S(2)}) copy-start(f32[512]{0:T(512)S(1)} %add_rsqrt_fusion) | copy-start | bytes 6148
  423.9 33.9 %copy-start.11 = (bf16[512,768]{0,1:T(8,128)(2,1)}, bf16[512,768]{0,1:T(8,128)(2,1)S(1)}, u32[]{:S(2)}) copy-start(bf16[512,768]{0,1:T(8,128)(2,1)S(1)} %copy.76) | copy-start | bytes 2359300
  471.1 177.4 %reduce-scatter.8.cloned.1.call-start = ((), (), s32[]{:S(2)}) async-start(), calls=%async_computation.8 | async-start | bytes 10027008 | tf_op jit(solution)/shard_map/reduce_scatter | solution.py:218
  504.7 324.3 %reduce-scatter.4.cloned.1.call-start = ((), (), s32[]{:S(2)}) async-start(), calls=%async_computation.6 | async-start | bytes 17547264 | tf_op jit(solution)/shard_map/reduce_scatter | solution.py:216
  550.0 10.8 %copy-start.12 = (bf16[512,768]{0,1:T(8,128)(2,1)S(1)}, bf16[512,768]{0,1:T(8,128)(2,1)}, u32[]{:S(2)}) copy-start(bf16[512,768]{0,1:T(8,128)(2,1)} %copy-done.11) | copy-start | bytes 2359300
  569.9 10.4 %copy-start.5 = (bf16[2,512,768]{2,1,0:T(8,128)(2,1)S(1)}, bf16[2,512,768]{2,1,0:T(8,128)(2,1)}, u32[]{:S(2)}) copy-start(bf16[2,512,768]{2,1,0:T(8,128)(2,1)} %param.10) | copy-start | bytes 4718596
  569.9 10.4 %copy-start.29 = (f32[768]{0:T(1024)S(1)}, f32[768]{0:T(1024)}, u32[]{:S(2)}) copy-start(f32[768]{0:T(1024)} %copy-done.28) | copy-start | bytes 9220
  569.9 10.4 %copy-start.33 = (bf16[512,768]{1,0:T(8,128)(2,1)S(1)}, bf16[512,768]{1,0:T(8,128)(2,1)}, u32[]{:S(2)}) copy-start(bf16[512,768]{1,0:T(8,128)(2,1)} %copy.85) | copy-start | bytes 2359300
  569.9 10.4 %copy-start.43 = (f32[512]{0:T(512)S(1)}, f32[512]{0:T(512)}, u32[]{:S(2)}) copy-start(f32[512]{0:T(512)} %copy-done.42) | copy-start | bytes 6148
  569.9 10.4 %copy-start.45 = (f32[512]{0:T(512)S(1)}, f32[512]{0:T(512)}, u32[]{:S(2)}) copy-start(f32[512]{0:T(512)} %copy-done.44) | copy-start | bytes 6148
  569.9 10.4 %copy-start.34 = (bf16[512,768]{1,0:T(8,128)(2,1)S(1)}, bf16[512,768]{1,0:T(8,128)(2,1)}, u32[]{:S(2)}) copy-start(bf16[512,768]{1,0:T(8,128)(2,1)} %copy.84) | copy-start | bytes 2359300
  569.9 10.4 %copy-start.35 = (bf16[512,768]{1,0:T(8,128)(2,1)S(1)}, bf16[512,768]{1,0:T(8,128)(2,1)}, u32[]{:S(2)}) copy-start(bf16[512,768]{1,0:T(8,128)(2,1)} %copy.83) | copy-start | bytes 2359300
  589.4 10.2 %copy-start.23 = (bf16[512,768]{1,0:T(8,128)(2,1)S(1)}, bf16[512,768]{1,0:T(8,128)(2,1)}, u32[]{:S(2)}) copy-start(bf16[512,768]{1,0:T(8,128)(2,1)} %copy.92) | copy-start | bytes 2359300
  589.4 10.2 %copy-start.25 = (bf16[512,768]{1,0:T(8,128)(2,1)S(1)}, bf16[512,768]{1,0:T(8,128)(2,1)}, u32[]{:S(2)}) copy-start(bf16[512,768]{1,0:T(8,128)(2,1)} %copy.91) | copy-start | bytes 2359300
  589.4 10.2 %copy-start.27 = (bf16[512,768]{1,0:T(8,128)(2,1)S(1)}, bf16[512,768]{1,0:T(8,128)(2,1)}, u32[]{:S(2)}) copy-start(bf16[512,768]{1,0:T(8,128)(2,1)} %copy.90) | copy-start | bytes 2359300
  612.6 294.4 %all-reduce.14.cloned.1.call-start = ((), (), s32[]{:S(2)}) async-start(), calls=%async_computation.9 | async-start | bytes 3538944 | tf_op jit(solution)/shard_map/psum | solution.py:224
  616.1 10.7 %slice-start = ((s8[4718592]{0:T(1024)(128)(4,1)}), s8[4194304]{0:T(1024)(128)(4,1)S(1)}, s32[]{:S(2)}) async-start(s8[4718592]{0:T(1024)(128)(4,1)} %bitcast.251), calls=%async_computation.10 | async-start | bytes 8388608
  (37 other events, 220.7 us)
Sparse Core Ops, SparseCore 0:
  10.3 41.7 all-gather.3
  54.4 66.1 all-gather.5
  125.6 173.7 all-gather.7
  471.2 62.3 reduce-scatter.5
  538.1 110.3 reduce-scatter.7
  652.7 176.3 reduce-scatter.3
  831.6 55.1 all-reduce.13
